TPU v7x, 32 devices: a whole 2x2x4 slice. The times are simulated.
32 devices in a mesh: groups: 2 (over x), ctx: 16 (over z, y, core).
Axes of the slice: x: 2, y: 2, z: 4, core: 2. Of those that a mesh axis runs over, the one named last changes fastest.
Arguments:
- hidden_rows: bfloat16 [16384, 4096], P(('groups', 'ctx')), parts along dimension 0, may hold values from -6 to 6
- positions: int32 [16384], P(('groups', 'ctx')), parts along dimension 0, may hold values from 0 to 32767
- owners: int32 [16384, 1], P(('groups', 'ctx')), parts along dimension 0, may hold values from 0 to 15; in each aligned block of 512 rows (0 to 511, 512 to 1023, ...) at most 64 rows name the same one
- lengths: int32 [8], P('groups'), parts along dimension 0, may hold values from 1 to 4096, 8192 in all
- queries: bfloat16 [32, 8192], P(('groups', 'ctx')), parts along dimension 0, may hold values from -400 to 400
- ln_gain: float32 [4096], replicated, may hold values from 0.1 to 1.9
- w_key: bfloat16 [4096, 512], replicated, may hold values from -0.09375 to 0.09375
- w_value: bfloat16 [4096, 512], replicated, may hold values from -0.09375 to 0.09375
- k_gain: float32 [128], replicated, may hold values from 0.1 to 1.9
Outputs:
- attended: bfloat16 [32, 8192], P(('groups', 'ctx')), parts along dimension 0
- key_cache: bfloat16 [32768, 512], P(('groups', 'ctx')), parts along dimension 0
- value_cache: bfloat16 [32768, 512], P(('groups', 'ctx')), parts along dimension 0
There are 2 independent parts, one for each index of `groups`. A program takes and returns all parts, laid end to end along the dimension named above; an argument that names none is the same for every part. Nothing has to cross between parts.
Inputs may be any that keep to these rules, and one draw needn't show every extreme that they name: `owners`: among the rows of one device at most 64 name the same shard, and in every draw some shard is named by exactly 64 rows of some device. The lengths sum to 8192; conversations follow one another in row order.
All inputs are finite; a program needn't handle non-finite values.
Results may differ from a plain program's by a relative error of at most 0.015.
The roundings to bfloat16 on the way count: a program that leaves them out, or rounds other values in their place, can miss the bound.
Values may be sent and summed in bfloat16 or wider, within the bound.
A program may use at most 128 MiB of HBM per device.

v0:
```python
import functools

import jax
import jax.numpy as jnp
import numpy as np
from jax import lax
from jax.experimental import pallas as pl
from jax.experimental.pallas import tpu as pltpu
from jax.sharding import PartitionSpec as P

EPSILON = 1e-06
THETA = 1000000.0
MASKED = -1e30
MESH = pl.DeviceIdType.MESH
F32 = jnp.float32
BF16 = jnp.bfloat16


def xor(a, b, n):
    out, bit = 0, 1
    while bit < n:
        p, q = (a // bit) % 2, (b // bit) % 2
        out = out + bit * (p + q - 2 * p * q)
        bit *= 2
    return out


def kernel(n, plane, cap, hd, x_ref, wk_ref, wv_ref, len_in, own_in, pos_in, freq_in, q_in, gain_in, kg_in,
           att_ref, key_ref, val_ref,
           x, w, normed, kv, onehot, pack, flat, mine, q_all, part, stat, pa, sa, mid_p, mid_s, pb, sb, turn,
           len_ref, own_ref, pos_ref, freq_ref, q_ref, gain_ref, kg_ref,
           small_sem, x_sem, w_sem, own_sem, kv_send, kv_recv, hop_send, hop_recv):
    me = lax.axis_index("ctx")
    grp = lax.axis_index("groups")
    lines = n // plane
    line, spot = me // plane, me % plane
    rows, width = x.shape
    heads = mine.shape[0]
    kvh = wk_ref.shape[1] // hd
    group = heads // kvh
    chunk = w.shape[2]
    per = wk_ref.shape[1] // chunk
    chunks = 2 * per

    def loop(count, body):
        def step(i, carry):
            body(i)
            return carry
        lax.fori_loop(1, count, step, 0)

    def every(body):
        loop(n, lambda i: body(xor(me, n - i, n)))

    barrier = pltpu.get_barrier_semaphore()
    every(lambda d: pl.semaphore_signal(barrier, inc=1, device_id=(grp, d), device_id_type=MESH))

    smalls = {}
    for i, (name, src, dst) in enumerate((
        ("q", q_in, q_ref), ("own", own_in, own_ref), ("gain", gain_in, gain_ref), ("len", len_in, len_ref),
        ("pos", pos_in, pos_ref), ("freq", freq_in, freq_ref), ("kg", kg_in, kg_ref),
    )):
        smalls[name] = pltpu.make_async_copy(src, dst, small_sem.at[i])
        smalls[name].start()
    x_parts = x_sem.shape[0]
    xr = rows // x_parts
    x_copies = [
        pltpu.make_async_copy(x_ref.at[pl.ds(i * xr, xr)], x.at[pl.ds(i * xr, xr)], x_sem.at[i])
        for i in range(x_parts)
    ]
    for copy in x_copies:
        copy.start()
    w_copies = []
    for c in range(chunks):
        src = wv_ref if c < per else wk_ref
        copy = pltpu.make_async_copy(src.at[:, pl.ds((c % per) * chunk, chunk)], w.at[c], w_sem.at[c])
        w_copies.append(copy)
    w_copies[0].start()

    smalls["q"].wait()
    for h in range(heads):
        flat[h:h + 1, :] = q_ref[:, h * hd:(h + 1) * hd].astype(F32)
    mine[...] = flat[...].astype(BF16)

    smalls["own"].wait()
    own = own_ref[...]
    named = jnp.where(lax.broadcasted_iota(jnp.int32, (n, rows), 0) == own, 1.0, 0.0)
    earlier = jnp.where(
        lax.broadcasted_iota(jnp.int32, (rows, rows), 0) < lax.broadcasted_iota(jnp.int32, (rows, rows), 1), 1.0, 0.0
    ).astype(BF16)
    before = jnp.dot(named.astype(BF16), earlier, preferred_element_type=F32)
    rank = jnp.sum(before * named, axis=0, keepdims=True)
    slot = own.astype(F32) * cap + rank
    slots = n * cap
    step = 128
    for b in range(slots // step):
        places = (lax.broadcasted_iota(jnp.int32, (step, rows), 0) + b * step).astype(F32)
        onehot[pl.ds(b * step, step), :] = jnp.where(places == slot, 1.0, 0.0).astype(BF16)

    def send(src, dst, s_sem, r_sem, d):
        pltpu.make_async_remote_copy(
            src_ref=src, dst_ref=dst, send_sem=s_sem, recv_sem=r_sem, device_id=(grp, d), device_id_type=MESH
        ).start()

    def whole(ref, sem):
        pltpu.make_async_copy(ref, ref, sem).wait()

    def on_line(body):
        loop(lines, lambda i: body(xor(line, lines - i, lines)))

    def on_plane(body):
        loop(plane, lambda i: body(xor(spot, plane - i, plane)))

    smalls["gain"].wait()
    gain = gain_ref[...]
    tile = 16
    for i in range(x_parts):
        x_copies[i].wait()

        def norm(t, carry):
            at = pl.ds(pl.multiple_of(i * xr + t * tile, tile), tile)
            wide = x[at, :].astype(F32)
            scale = lax.rsqrt(jnp.mean(wide * wide, axis=-1, keepdims=True) + EPSILON)
            normed[at, :] = (wide * scale * gain).astype(BF16)
            return carry
        lax.fori_loop(0, xr // tile, norm, 0, unroll=True)
        if i == 0:
            for copy in w_copies[1:]:
                copy.start()

    own_copies = []

    def ship(c):
        out_ref = val_ref if c < per else key_ref
        cols = pl.ds((c % per) * chunk, chunk)
        packed = jnp.dot(onehot[...], kv[c], preferred_element_type=F32)
        pack[c] = packed.reshape(n, cap, chunk).astype(BF16)
        every(lambda d: send(pack.at[c, d], out_ref.at[me, :, cols], kv_send.at[c], kv_recv.at[c], d))
        copy = pltpu.make_async_copy(pack.at[c, me], out_ref.at[me, :, cols], own_sem.at[c])
        copy.start()
        own_copies.append(copy)

    def project(c):
        w_copies[c].wait()
        raw = jnp.dot(normed[...], w[c], preferred_element_type=F32)
        if c < per:
            kv[c] = raw.astype(BF16)
            return
        for h in range(chunk // hd):
            head = raw[:, h * hd:(h + 1) * hd]
            head = head * lax.rsqrt(jnp.mean(head * head, axis=-1, keepdims=True) + EPSILON) * kg_ref[...]
            turned = pltpu.roll(head, hd // 2, 1)
            kv[c, :, h * hd:(h + 1) * hd] = (head * turn[0] + turned * turn[1]).astype(BF16)

    project(0)
    pl.semaphore_wait(barrier, n - 1)
    on_line(lambda j: send(mine, q_all.at[line, spot], hop_send.at[0], hop_recv.at[0], j * plane + spot))
    q_all[line, spot] = mine[...]
    ship(0)
    for c in range(1, per):
        project(c)
        ship(c)
    whole(q_all.at[pl.ds(0, lines - 1), 0], hop_recv.at[0])
    on_plane(
        lambda j: send(q_all.at[:, spot], q_all.at[:, spot], hop_send.at[1], hop_recv.at[1], line * plane + j)
    )

    for name in ("len", "pos", "freq", "kg"):
        smalls[name].wait()
    angles = freq_ref[...] * pos_ref[...].astype(F32)
    cosine, sine = jnp.cos(angles), jnp.sin(angles)
    turn[0] = jnp.concatenate([cosine, cosine], axis=0).T
    turn[1] = jnp.concatenate([-sine, sine], axis=0).T
    for c in range(per, chunks):
        project(c)
        if c < chunks - 1:
            ship(c)

    row = me * rows + lax.broadcasted_iota(jnp.int32, (1, rows), 1)
    convs = len_ref.shape[0]
    row_conv, end = jnp.zeros((1, rows), jnp.int32), 0
    for j in range(convs):
        end = end + len_ref[j]
        row_conv = row_conv + jnp.where(row >= end, 1, 0)

    whole(q_all.at[:, pl.ds(0, plane - 1)], hop_recv.at[1])
    span = min(lines, max(1, 16 // plane))
    lined = span * plane * group
    per_conv = n // convs
    scale = 1.0 / (hd ** 0.5)
    in_chunk = chunk // hd

    def attend(b, carry):
        first = b * span * plane
        at = pl.ds(b * span, span)
        asks = (first + lax.broadcasted_iota(jnp.int32, (lined, rows), 0) // group) // per_conv
        allowed = asks == row_conv
        lane = lax.broadcasted_iota(jnp.int32, (lined, 128), 1)
        logs = jnp.zeros((lined, 128), F32)
        for k in range(kvh):
            q = q_all[at, :, k * group:(k + 1) * group, :].reshape(lined, hd)
            cols = slice((k % in_chunk) * hd, (k % in_chunk + 1) * hd)
            keys = kv[per + k // in_chunk, :, cols]
            values = kv[k // in_chunk, :, cols]
            scores = lax.dot_general(q, keys, (((1,), (1,)), ((), ())), preferred_element_type=F32) * scale
            scores = jnp.where(allowed, scores, MASKED)
            peak = jnp.max(scores, axis=-1, keepdims=True)
            expos = jnp.exp(scores - peak)
            sums = jnp.sum(expos, axis=-1, keepdims=True)
            mixed = jnp.dot(expos.astype(BF16), values, preferred_element_type=F32) / sums
            part[at, :, k * group:(k + 1) * group, :] = mixed.reshape(span, plane, group, hd).astype(BF16)
            logs = jnp.where(lane == k, peak + jnp.log(sums), logs)
        stat[at] = logs.reshape(span, plane, group, 128)
        return carry

    lax.fori_loop(0, lines // span, attend, 0)

    def give(j):
        send(part.at[:, j], pa.at[spot], hop_send.at[2], hop_recv.at[2], line * plane + j)
        send(stat.at[:, j], sa.at[spot], hop_send.at[3], hop_recv.at[3], line * plane + j)

    on_plane(give)
    pa[spot] = part[:, spot]
    sa[spot] = stat[:, spot]

    def merge(count, p_at, s_at):
        top = lax.fori_loop(0, count, lambda s, t: jnp.maximum(t, s_at(s)), jnp.full((group, 128), MASKED, F32))

        def add(s, carry):
            below, sums = carry
            factor = jnp.exp(s_at(s) - top)
            sums = tuple(sums[k] + factor[:, k:k + 1] * p_at(s, k).astype(F32) for k in range(kvh))
            return below + factor, sums

        zeros = jnp.zeros((group, 128), F32), tuple(jnp.zeros((group, hd), F32) for _ in range(kvh))
        below, sums = lax.fori_loop(0, count, add, zeros)
        return [(sums[k] / below[:, k:k + 1]).astype(BF16) for k in range(kvh)], top + jnp.log(below)

    whole(pa.at[pl.ds(0, plane - 1)], hop_recv.at[2])
    whole(sa.at[pl.ds(0, plane - 1)], hop_recv.at[3])

    def halfway(l, carry):
        mixed, logs = merge(
            plane, lambda s, k: pa[s, l, k * group:(k + 1) * group, :], lambda s: sa[s, l]
        )
        for k in range(kvh):
            mid_p[l, k * group:(k + 1) * group, :] = mixed[k]
        mid_s[l] = logs
        return carry

    lax.fori_loop(0, lines, halfway, 0)

    def give_on(j):
        send(mid_p.at[j], pb.at[line], hop_send.at[4], hop_recv.at[4], j * plane + spot)
        send(mid_s.at[j], sb.at[line], hop_send.at[5], hop_recv.at[5], j * plane + spot)

    on_line(give_on)
    pb[line] = mid_p[line]
    sb[line] = mid_s[line]
    ship(chunks - 1)
    whole(pb.at[pl.ds(0, lines - 1)], hop_recv.at[4])
    whole(sb.at[pl.ds(0, lines - 1)], hop_recv.at[5])
    mixed, _ = merge(lines, lambda s, k: pb[s, k * group:(k + 1) * group, :], lambda s: sb[s])
    for k in range(kvh):
        flat[k * group:(k + 1) * group, :] = mixed[k].astype(F32)
    for h in range(heads):
        att_ref[:, h * hd:(h + 1) * hd] = flat[h:h + 1, :].astype(BF16)

    whole(q_all.at[pl.ds(0, lines - 1), 0], hop_send.at[0])
    whole(q_all.at[:, pl.ds(0, plane - 1)], hop_send.at[1])
    whole(pa.at[pl.ds(0, plane - 1)], hop_send.at[2])
    whole(sa.at[pl.ds(0, plane - 1)], hop_send.at[3])
    whole(pb.at[pl.ds(0, lines - 1)], hop_send.at[4])
    whole(sb.at[pl.ds(0, lines - 1)], hop_send.at[5])
    for c in range(chunks):
        whole(pack.at[c, pl.ds(0, n - 1)], kv_send.at[c])
        whole(pack.at[c, pl.ds(0, n - 1)], kv_recv.at[c])
        own_copies[c].wait()


def on_device(hidden_rows, positions, owners, lengths, queries, ln_gain, w_key, w_value, k_gain):
    count, width = hidden_rows.shape
    n = lax.axis_size("ctx")
    hd = k_gain.shape[0]
    kv_width = w_key.shape[1]
    heads = queries.shape[1] // hd
    kvh = kv_width // hd
    group = heads // kvh
    cap = max(2, 2 * count // n)
    plane = 1
    while plane * plane < n:
        plane *= 2
    lines = n // plane
    freqs = np.float64(THETA) ** (-(np.arange(hd // 2) * 2.0) / hd)
    freqs = jnp.asarray(freqs.astype(np.float32)[:, None])

    chunk = 2 * hd
    chunks = 2 * kv_width // chunk
    vmem = pl.BlockSpec(memory_space=pltpu.VMEM)
    dma = pltpu.SemaphoreType.DMA
    attended, key_cache, value_cache = pl.pallas_call(
        functools.partial(kernel, n, plane, cap, hd),
        out_shape=(
            pltpu.VMEM((1, heads * hd), BF16),
            pltpu.VMEM((n, cap, kv_width), BF16),
            pltpu.VMEM((n, cap, kv_width), BF16),
        ),
        in_specs=[pl.BlockSpec(memory_space=pltpu.HBM)] * 10,
        out_specs=(vmem, vmem, vmem),
        scratch_shapes=[
            pltpu.VMEM((count, width), BF16),
            pltpu.VMEM((chunks, width, chunk), BF16),
            pltpu.VMEM((count, width), BF16),
            pltpu.VMEM((chunks, count, chunk), BF16),
            pltpu.VMEM((n * cap, count), BF16),
            pltpu.VMEM((chunks, n, cap, chunk), BF16),
            pltpu.VMEM((heads, hd), F32),
            pltpu.VMEM((heads, hd), BF16),
            pltpu.VMEM((lines, plane, heads, hd), BF16),
            pltpu.VMEM((lines, plane, heads, hd), BF16),
            pltpu.VMEM((lines, plane, group, 128), F32),
            pltpu.VMEM((plane, lines, heads, hd), BF16),
            pltpu.VMEM((plane, lines, group, 128), F32),
            pltpu.VMEM((lines, heads, hd), BF16),
            pltpu.VMEM((lines, group, 128), F32),
            pltpu.VMEM((lines, heads, hd), BF16),
            pltpu.VMEM((lines, group, 128), F32),
            pltpu.VMEM((2, count, hd), F32),
            pltpu.SMEM(lengths.shape, jnp.int32),
            pltpu.VMEM((1, count), jnp.int32),
            pltpu.VMEM((1, count), jnp.int32),
            pltpu.VMEM(freqs.shape, F32),
            pltpu.VMEM(queries.shape, BF16),
            pltpu.VMEM((1, width), F32),
            pltpu.VMEM((1, hd), F32),
            dma((7,)),
            dma((4,)),
            dma((chunks,)),
            dma((chunks,)),
            dma((chunks,)),
            dma((chunks,)),
            dma((6,)),
            dma((6,)),
        ],
        compiler_params=pltpu.CompilerParams(
            collective_id=0, has_side_effects=True, vmem_limit_bytes=60 * 1024 * 1024
        ),
        name="restore_attend",
    )(
        hidden_rows, w_key, w_value, lengths, owners.reshape(1, count), positions.reshape(1, count), freqs, queries,
        ln_gain.reshape(1, width), k_gain.reshape(1, hd),
    )
    return attended, key_cache.reshape(n * cap, kv_width), value_cache.reshape(n * cap, kv_width)


def solution(mesh):
    rows = P(("groups", "ctx"), None)
    return jax.shard_map(
        on_device,
        mesh=mesh,
        in_specs=(rows, P(("groups", "ctx")), rows, P("groups"), rows, P(), P(), P(), P()),
        out_specs=(rows, rows, rows),
        check_vma=False,
    )
```

profile of v0, /device:TPU:0, one launch (start us, length us, event | category | flops | bytes accessed | tf_op | source)
XLA Modules:
  0.0 63.6 jit_solution(1484623722182913190)
XLA Ops:
  0.6 60.4 %restore_attend.1 = (bf16[1,8192]{1,0:T(2,128)(2,1)S(1)}, bf16[16,64,512]{2,1,0:T(8,128)(2,1)S(1)}, bf16[16,64,512]{2,1,0:T(8,128)(2,1)S(1)}) custom-call(bf16[512,4096]{1,0:T(8,128)(2,1)} %x_ref.1, bf16[4096,512]{1,0:T(8,128)(2,1)} %wk_ref.1, bf16[4096,512]{1,0:T(8,128)(2,1)} %wv_ref.1, s32[4]{0:T(128)} %len_in.1, s32[1,512]{1,0:T(1,128)} %bitcast.9, ...), custom_call_target="tpu_custom_call" | custom-call | tf_op jit(solution)/shard_map/restore_attend/pallas_call | solution.py:300
  61.0 0.6 copy.16
  61.6 1.0 %copy.17 = bf16[1024,512]{1,0:T(8,128)(2,1)} copy(bf16[1024,512]{1,0:T(8,128)(2,1)S(1)} %bitcast.7) | data formatting | bytes 2097152
  62.6 1.0 %copy.18 = bf16[1024,512]{1,0:T(8,128)(2,1)} copy(bf16[1024,512]{1,0:T(8,128)(2,1)S(1)} %bitcast.6) | data formatting | bytes 2097152
where the time goes:
time: 63.7 us; the launch traced here: 63.6 us
  Pallas kernels  60.4 us (95%)
  local copies, waits for them, and re-layouts  2.56 us (4%)
  between operations  0.64 us (1%)
    pallas_call x1, Pallas kernels, on_device(): pl.pallas_call(functools.partial(kernel, n, plane, cap, hd), out_shape=(p...  60.4 us
    unnamed x3, local copies, waits for them, and re-layouts  2.56 us

commit v1 on v0

--- a/solution.py
+++ b/solution.py
@@ -23,6 +23,360 @@
         out = out + bit * (p + q - 2 * p * q)
         bit *= 2
     return out
+
+
+def fast_kernel(n, plane, cap, hd, fill, x_ref, wk_ref, wv_ref, len_in, own_in, pos_in, freq_in, q_in, gain_in, kg_in,
+                att_ref, key_ref, val_ref, over_ref,
+                x, w, normed, kv, onehot, pick, pack, far, gate, place, ward, flat, mine, q_all, part, stat, pa, sa,
+                mid_p, mid_s, pb, sb, turn, goes, comes, over, overs,
+                len_ref, own_ref, pos_ref, freq_ref, q_ref, gain_ref, kg_ref,
+                small_sem, x_sem, w_sem, own_sem, kv_send, kv_recv, hop_send, hop_recv,
+                far_send, gate_recv, ward_send, ward_recv, note_send, note_recv):
+    me = lax.axis_index("ctx")
+    grp = lax.axis_index("groups")
+    grps = lax.axis_size("groups")
+    lines = n // plane
+    line, spot = me // plane, me % plane
+    half = n // 2
+    deep = lines // 2
+    side = me // half
+    near = side * half
+    gate_line = side * (deep - 1) + (1 - side) * deep
+    my_gate = gate_line * plane + spot
+    is_gate = line == (1 - side) * (deep - 1) + side * deep
+    rows, width = x.shape
+    heads = mine.shape[0]
+    kvh = wk_ref.shape[1] // hd
+    group = heads // kvh
+    chunk = w.shape[2]
+    per = wk_ref.shape[1] // chunk
+    chunks = 2 * per
+    hopped = gate.shape[0]
+
+    def loop(count, body):
+        def step(i, carry):
+            body(i)
+            return carry
+        lax.fori_loop(1, count, step, 0)
+
+    def every(body):
+        loop(n, lambda i: body(xor(me, n - i, n)))
+
+    def beside(body):
+        loop(half, lambda i: body(xor(me, half - i, n)))
+
+    def others(body):
+        loop(grps, lambda i: body((grp + i) % grps, i - 1))
+
+    barrier = pltpu.get_barrier_semaphore()
+    every(lambda d: pl.semaphore_signal(barrier, inc=1, device_id=(grp, d), device_id_type=MESH))
+    others(lambda g, i: pl.semaphore_signal(barrier, inc=1, device_id=(g, me), device_id_type=MESH))
+
+    smalls = {}
+    for i, (name, src, dst) in enumerate((
+        ("q", q_in, q_ref), ("own", own_in, own_ref), ("gain", gain_in, gain_ref), ("len", len_in, len_ref),
+        ("pos", pos_in, pos_ref), ("freq", freq_in, freq_ref), ("kg", kg_in, kg_ref),
+    )):
+        smalls[name] = pltpu.make_async_copy(src, dst, small_sem.at[i])
+        smalls[name].start()
+    x_parts = x_sem.shape[0]
+    xr = rows // x_parts
+    x_copies = [
+        pltpu.make_async_copy(x_ref.at[pl.ds(i * xr, xr)], x.at[pl.ds(i * xr, xr)], x_sem.at[i])
+        for i in range(x_parts)
+    ]
+    for copy in x_copies:
+        copy.start()
+    w_copies = []
+    for c in range(chunks):
+        src = wv_ref if c < per else wk_ref
+        copy = pltpu.make_async_copy(src.at[:, pl.ds((c % per) * chunk, chunk)], w.at[c], w_sem.at[c])
+        w_copies.append(copy)
+    w_copies[0].start()
+
+    smalls["q"].wait()
+    for h in range(heads):
+        flat[h:h + 1, :] = q_ref[:, h * hd:(h + 1) * hd].astype(F32)
+    mine[...] = flat[...].astype(BF16)
+
+    smalls["own"].wait()
+    own = own_ref[...]
+    named = jnp.where(lax.broadcasted_iota(jnp.int32, (n, rows), 0) == own, 1.0, 0.0)
+    afar = jnp.where(own // half == side, 0.0, 1.0)
+    marks = jnp.concatenate([named, jnp.broadcast_to(afar, (16, rows))], axis=0)
+    earlier = jnp.where(
+        lax.broadcasted_iota(jnp.int32, (rows, rows), 0) < lax.broadcasted_iota(jnp.int32, (rows, rows), 1), 1.0, 0.0
+    ).astype(BF16)
+    before = jnp.dot(marks.astype(BF16), earlier, preferred_element_type=F32)
+    rank = jnp.sum(before[:n] * named, axis=0, keepdims=True)
+    slot = own.astype(F32) * cap + rank
+    slots = n * cap
+    step = 128
+    for b in range(slots // step):
+        places = (lax.broadcasted_iota(jnp.int32, (step, rows), 0) + b * step).astype(F32)
+        onehot[pl.ds(b * step, step), :] = jnp.where(places == slot, 1.0, 0.0).astype(BF16)
+    seat = jnp.where(afar > 0.0, before[n:n + 1], -1.0)
+    for b in range(fill // step):
+        places = (lax.broadcasted_iota(jnp.int32, (step, rows), 0) + b * step).astype(F32)
+        pick[pl.ds(b * step, step), :] = jnp.where(places == seat, 1.0, 0.0).astype(BF16)
+    there = own.astype(F32) + 1.0
+    facts = jnp.where(lax.broadcasted_iota(jnp.int32, (16, rows), 0) == 0, there, rank).astype(BF16)
+    told = lax.dot_general(facts, pick[...], (((1,), (1,)), ((), ())), preferred_element_type=F32)
+    goes[...] = (told[0:1] - 1.0 - ((1 - side) * half).astype(F32)) * cap + told[1:2]
+    full = jnp.where(jnp.sum(afar, axis=1, keepdims=True) > fill, 1.0, 0.0)
+    over[...] = jnp.broadcast_to(full, over.shape)
+
+    def send(src, dst, s_sem, r_sem, d):
+        pltpu.make_async_remote_copy(
+            src_ref=src, dst_ref=dst, send_sem=s_sem, recv_sem=r_sem, device_id=(grp, d), device_id_type=MESH
+        ).start()
+
+    def tell(g, i):
+        pltpu.make_async_remote_copy(
+            src_ref=over, dst_ref=overs.at[i], send_sem=note_send.at[1], recv_sem=note_recv.at[1],
+            device_id=(g, me), device_id_type=MESH
+        ).start()
+
+    def whole(ref, sem):
+        pltpu.make_async_copy(ref, ref, sem).wait()
+
+    def on_line(body):
+        loop(lines, lambda i: body(xor(line, lines - i, lines)))
+
+    def on_plane(body):
+        loop(plane, lambda i: body(xor(spot, plane - i, plane)))
+
+    smalls["gain"].wait()
+    gain = gain_ref[...]
+    tile = 16
+    for i in range(x_parts):
+        x_copies[i].wait()
+
+        def norm(t, carry):
+            at = pl.ds(pl.multiple_of(i * xr + t * tile, tile), tile)
+            wide = x[at, :].astype(F32)
+            scale = lax.rsqrt(jnp.mean(wide * wide, axis=-1, keepdims=True) + EPSILON)
+            normed[at, :] = (wide * scale * gain).astype(BF16)
+            return carry
+        lax.fori_loop(0, xr // tile, norm, 0, unroll=True)
+        if i == 0:
+            for copy in w_copies[1:]:
+                copy.start()
+
+    own_copies = []
+
+    def target(c):
+        return val_ref if c < per else key_ref, pl.ds((c % per) * chunk, chunk)
+
+    def keep(c):
+        out_ref, cols = target(c)
+        copy = pltpu.make_async_copy(pack.at[c, me], out_ref.at[me, :, cols], own_sem.at[c])
+        copy.start()
+        own_copies.append(copy)
+
+    def hop(c):
+        out_ref, cols = target(c)
+        far[c] = jnp.dot(pick[...], kv[c], preferred_element_type=F32).astype(BF16)
+        send(far.at[c], gate.at[c, line % deep], far_send.at[c], gate_recv.at[c], my_gate)
+        at = pl.ds(pl.multiple_of(near * cap, half * cap), half * cap)
+        packed = jnp.dot(onehot[at, :], kv[c], preferred_element_type=F32)
+        pack[c, pl.ds(near, half)] = packed.reshape(half, cap, chunk).astype(BF16)
+        beside(lambda d: send(pack.at[c, d], out_ref.at[me, :, cols], kv_send.at[c], kv_recv.at[c], d))
+        keep(c)
+
+    def ship(c):
+        out_ref, cols = target(c)
+        packed = jnp.dot(onehot[...], kv[c], preferred_element_type=F32)
+        pack[c] = packed.reshape(n, cap, chunk).astype(BF16)
+        every(lambda d: send(pack.at[c, d], out_ref.at[me, :, cols], kv_send.at[c], kv_recv.at[c], d))
+        keep(c)
+
+    def forward(c):
+        out_ref, cols = target(c)
+
+        @pl.when(is_gate)
+        def _():
+            whole(gate.at[c], gate_recv.at[c])
+            if c == 0:
+                whole(comes, note_recv.at[0])
+                for j in range(deep):
+                    for b in range(half * cap // step):
+                        places = (lax.broadcasted_iota(jnp.int32, (step, fill), 0) + b * step).astype(F32)
+                        place[j, pl.ds(b * step, step), :] = jnp.where(places == comes[j], 1.0, 0.0).astype(BF16)
+            for j in range(deep):
+                source = ((1 - side) * deep + j) * plane + spot
+                spread = jnp.dot(place[j], gate[c, j], preferred_element_type=F32)
+                ward[c, j] = spread.reshape(half, cap, chunk).astype(BF16)
+                beside(lambda d: send(
+                    ward.at[c, j, d - near], out_ref.at[source, :, cols], ward_send.at[c], ward_recv.at[c], d))
+                out_ref[source, :, cols] = ward[c, j, me - near]
+
+    def project(c):
+        w_copies[c].wait()
+        raw = jnp.dot(normed[...], w[c], preferred_element_type=F32)
+        if c < per:
+            kv[c] = raw.astype(BF16)
+            return
+        for h in range(chunk // hd):
+            head = raw[:, h * hd:(h + 1) * hd]
+            head = head * lax.rsqrt(jnp.mean(head * head, axis=-1, keepdims=True) + EPSILON) * kg_ref[...]
+            turned = pltpu.roll(head, hd // 2, 1)
+            kv[c, :, h * hd:(h + 1) * hd] = (head * turn[0] + turned * turn[1]).astype(BF16)
+
+    project(0)
+    pl.semaphore_wait(barrier, n - 1 + grps - 1)
+    on_line(lambda j: send(mine, q_all.at[line, spot], hop_send.at[0], hop_recv.at[0], j * plane + spot))
+    send(goes, comes.at[line % deep], note_send.at[0], note_recv.at[0], my_gate)
+    others(tell)
+    q_all[line, spot] = mine[...]
+    hop(0)
+    for c in range(1, per):
+        project(c)
+        hop(c)
+    whole(q_all.at[pl.ds(0, lines - 1), 0], hop_recv.at[0])
+    on_plane(
+        lambda j: send(q_all.at[:, spot], q_all.at[:, spot], hop_send.at[1], hop_recv.at[1], line * plane + j)
+    )
+
+    for name in ("len", "pos", "freq", "kg"):
+        smalls[name].wait()
+    angles = freq_ref[...] * pos_ref[...].astype(F32)
+    cosine, sine = jnp.cos(angles), jnp.sin(angles)
+    turn[0] = jnp.concatenate([cosine, cosine], axis=0).T
+    turn[1] = jnp.concatenate([-sine, sine], axis=0).T
+    for c in range(per, chunks):
+        project(c)
+        if c < hopped:
+            hop(c)
+
+    row = me * rows + lax.broadcasted_iota(jnp.int32, (1, rows), 1)
+    convs = len_ref.shape[0]
+    row_conv, end = jnp.zeros((1, rows), jnp.int32), 0
+    for j in range(convs):
+        end = end + len_ref[j]
+        row_conv = row_conv + jnp.where(row >= end, 1, 0)
+
+    whole(overs, note_recv.at[1])
+    flag = over[0:1, :]
+    for i in range(overs.shape[0]):
+        flag = jnp.maximum(flag, overs[i, 0:1, :])
+
+    whole(q_all.at[:, pl.ds(0, plane - 1)], hop_recv.at[1])
+    span = min(lines, max(1, 16 // plane))
+    lined = span * plane * group
+    per_conv = n // convs
+    scale = 1.0 / (hd ** 0.5)
+    in_chunk = chunk // hd
+
+    def attend(b, carry):
+        first = b * span * plane
+        at = pl.ds(b * span, span)
+        asks = (first + lax.broadcasted_iota(jnp.int32, (lined, rows), 0) // group) // per_conv
+        allowed = asks == row_conv
+        lane = lax.broadcasted_iota(jnp.int32, (lined, 128), 1)
+        logs = jnp.where(lane == 127, flag, 0.0)
+        for k in range(kvh):
+            q = q_all[at, :, k * group:(k + 1) * group, :].reshape(lined, hd)
+            cols = slice((k % in_chunk) * hd, (k % in_chunk + 1) * hd)
+            keys = kv[per + k // in_chunk, :, cols]
+            values = kv[k // in_chunk, :, cols]
+            scores = lax.dot_general(q, keys, (((1,), (1,)), ((), ())), preferred_element_type=F32) * scale
+            scores = jnp.where(allowed, scores, MASKED)
+            peak = jnp.max(scores, axis=-1, keepdims=True)
+            expos = jnp.exp(scores - peak)
+            sums = jnp.sum(expos, axis=-1, keepdims=True)
+            mixed = jnp.dot(expos.astype(BF16), values, preferred_element_type=F32) / sums
+            part[at, :, k * group:(k + 1) * group, :] = mixed.reshape(span, plane, group, hd).astype(BF16)
+            logs = jnp.where(lane == k, peak + jnp.log(sums), logs)
+        stat[at] = logs.reshape(span, plane, group, 128)
+        return carry
+
+    lax.fori_loop(0, lines // span, attend, 0)
+
+    def give(j):
+        send(part.at[:, j], pa.at[spot], hop_send.at[2], hop_recv.at[2], line * plane + j)
+        send(stat.at[:, j], sa.at[spot], hop_send.at[3], hop_recv.at[3], line * plane + j)
+
+    on_plane(give)
+    pa[spot] = part[:, spot]
+    sa[spot] = stat[:, spot]
+    forward(0)
+
+    def merge(count, p_at, s_at):
+        top = lax.fori_loop(0, count, lambda s, t: jnp.maximum(t, s_at(s)), jnp.full((group, 128), MASKED, F32))
+
+        def add(s, carry):
+            below, sums = carry
+            factor = jnp.exp(s_at(s) - top)
+            sums = tuple(sums[k] + factor[:, k:k + 1] * p_at(s, k).astype(F32) for k in range(kvh))
+            return below + factor, sums
+
+        zeros = jnp.zeros((group, 128), F32), tuple(jnp.zeros((group, hd), F32) for _ in range(kvh))
+        below, sums = lax.fori_loop(0, count, add, zeros)
+        lane = lax.broadcasted_iota(jnp.int32, (group, 128), 1)
+        logs = jnp.where(lane == 127, top, top + jnp.log(below))
+        return [(sums[k] / below[:, k:k + 1]).astype(BF16) for k in range(kvh)], logs
+
+    whole(pa.at[pl.ds(0, plane - 1)], hop_recv.at[2])
+    whole(sa.at[pl.ds(0, plane - 1)], hop_recv.at[3])
+
+    def halfway(l, carry):
+        mixed, logs = merge(
+            plane, lambda s, k: pa[s, l, k * group:(k + 1) * group, :], lambda s: sa[s, l]
+        )
+        for k in range(kvh):
+            mid_p[l, k * group:(k + 1) * group, :] = mixed[k]
+        mid_s[l] = logs
+        return carry
+
+    lax.fori_loop(0, lines, halfway, 0)
+
+    def give_on(j):
+        send(mid_p.at[j], pb.at[line], hop_send.at[4], hop_recv.at[4], j * plane + spot)
+        send(mid_s.at[j], sb.at[line], hop_send.at[5], hop_recv.at[5], j * plane + spot)
+
+    on_line(give_on)
+    pb[line] = mid_p[line]
+    sb[line] = mid_s[line]
+    for c in range(hopped, chunks):
+        ship(c)
+    for c in range(1, hopped):
+        forward(c)
+    whole(pb.at[pl.ds(0, lines - 1)], hop_recv.at[4])
+    whole(sb.at[pl.ds(0, lines - 1)], hop_recv.at[5])
+    mixed, logs = merge(lines, lambda s, k: pb[s, k * group:(k + 1) * group, :], lambda s: sb[s])
+    lane = lax.broadcasted_iota(jnp.int32, (group, 128), 1)
+    over_ref[0] = jnp.max(jnp.where(lane == 127, logs, 0.0))
+    for k in range(kvh):
+        flat[k * group:(k + 1) * group, :] = mixed[k].astype(F32)
+    for h in range(heads):
+        att_ref[:, h * hd:(h + 1) * hd] = flat[h:h + 1, :].astype(BF16)
+
+    whole(q_all.at[pl.ds(0, lines - 1), 0], hop_send.at[0])
+    whole(q_all.at[:, pl.ds(0, plane - 1)], hop_send.at[1])
+    whole(pa.at[pl.ds(0, plane - 1)], hop_send.at[2])
+    whole(sa.at[pl.ds(0, plane - 1)], hop_send.at[3])
+    whole(pb.at[pl.ds(0, lines - 1)], hop_send.at[4])
+    whole(sb.at[pl.ds(0, lines - 1)], hop_send.at[5])
+    whole(goes, note_send.at[0])
+    whole(overs, note_send.at[1])
+    for c in range(chunks):
+        count = half - 1 if c < hopped else n - 1
+        whole(pack.at[c, pl.ds(0, count)], kv_send.at[c])
+        whole(pack.at[c, pl.ds(0, count)], kv_recv.at[c])
+        own_copies[c].wait()
+        if c < hopped:
+            whole(far.at[c], far_send.at[c])
+
+            @pl.when(is_gate)
+            def _():
+                for j in range(deep):
+                    whole(pack.at[c, pl.ds(0, half - 1)], ward_send.at[c])
+                whole(pack.at[c, pl.ds(0, (plane - 1) * deep)], ward_recv.at[c])
+
+            @pl.when(jnp.logical_not(is_gate))
+            def _():
+                whole(pack.at[c, pl.ds(0, plane * deep)], ward_recv.at[c])
 
 
 def kernel(n, plane, cap, hd, x_ref, wk_ref, wv_ref, len_in, own_in, pos_in, freq_in, q_in, gain_in, kg_in,
@@ -280,6 +634,7 @@
 def on_device(hidden_rows, positions, owners, lengths, queries, ln_gain, w_key, w_value, k_gain):
     count, width = hidden_rows.shape
     n = lax.axis_size("ctx")
+    grps = lax.axis_size("groups")
     hd = k_gain.shape[0]
     kv_width = w_key.shape[1]
     heads = queries.shape[1] // hd
@@ -290,64 +645,95 @@
     while plane * plane < n:
         plane *= 2
     lines = n // plane
+    half, deep = n // 2, lines // 2
+    fill = 3 * count // 4
     freqs = np.float64(THETA) ** (-(np.arange(hd // 2) * 2.0) / hd)
     freqs = jnp.asarray(freqs.astype(np.float32)[:, None])
 
     chunk = 2 * hd
     chunks = 2 * kv_width // chunk
+    hopped = chunks - 1
     vmem = pl.BlockSpec(memory_space=pltpu.VMEM)
     dma = pltpu.SemaphoreType.DMA
-    attended, key_cache, value_cache = pl.pallas_call(
-        functools.partial(kernel, n, plane, cap, hd),
-        out_shape=(
-            pltpu.VMEM((1, heads * hd), BF16),
-            pltpu.VMEM((n, cap, kv_width), BF16),
-            pltpu.VMEM((n, cap, kv_width), BF16),
-        ),
+    caches = pltpu.VMEM((n, cap, kv_width), BF16)
+    inputs = (
+        hidden_rows, w_key, w_value, lengths, owners.reshape(1, count), positions.reshape(1, count), freqs, queries,
+        ln_gain.reshape(1, width), k_gain.reshape(1, hd),
+    )
+    loaded = [
+        pltpu.SMEM(lengths.shape, jnp.int32),
+        pltpu.VMEM((1, count), jnp.int32),
+        pltpu.VMEM((1, count), jnp.int32),
+        pltpu.VMEM(freqs.shape, F32),
+        pltpu.VMEM(queries.shape, BF16),
+        pltpu.VMEM((1, width), F32),
+        pltpu.VMEM((1, hd), F32),
+    ]
+    spread = [
+        pltpu.VMEM((heads, hd), F32),
+        pltpu.VMEM((heads, hd), BF16),
+        pltpu.VMEM((lines, plane, heads, hd), BF16),
+        pltpu.VMEM((lines, plane, heads, hd), BF16),
+        pltpu.VMEM((lines, plane, group, 128), F32),
+        pltpu.VMEM((plane, lines, heads, hd), BF16),
+        pltpu.VMEM((plane, lines, group, 128), F32),
+        pltpu.VMEM((lines, heads, hd), BF16),
+        pltpu.VMEM((lines, group, 128), F32),
+        pltpu.VMEM((lines, heads, hd), BF16),
+        pltpu.VMEM((lines, group, 128), F32),
+        pltpu.VMEM((2, count, hd), F32),
+    ]
+    big = [
+        pltpu.VMEM((count, width), BF16),
+        pltpu.VMEM((chunks, width, chunk), BF16),
+        pltpu.VMEM((count, width), BF16),
+        pltpu.VMEM((chunks, count, chunk), BF16),
+        pltpu.VMEM((n * cap, count), BF16),
+    ]
+    pack = pltpu.VMEM((chunks, n, cap, chunk), BF16)
+    sems = [dma((7,)), dma((4,)), dma((chunks,)), dma((chunks,)), dma((chunks,)), dma((chunks,)), dma((6,)), dma((6,))]
+
+    attended, key_cache, value_cache, over = pl.pallas_call(
+        functools.partial(fast_kernel, n, plane, cap, hd, fill),
+        out_shape=(pltpu.VMEM((1, heads * hd), BF16), caches, caches, pltpu.SMEM((1,), F32)),
         in_specs=[pl.BlockSpec(memory_space=pltpu.HBM)] * 10,
-        out_specs=(vmem, vmem, vmem),
-        scratch_shapes=[
-            pltpu.VMEM((count, width), BF16),
-            pltpu.VMEM((chunks, width, chunk), BF16),
-            pltpu.VMEM((count, width), BF16),
-            pltpu.VMEM((chunks, count, chunk), BF16),
-            pltpu.VMEM((n * cap, count), BF16),
-            pltpu.VMEM((chunks, n, cap, chunk), BF16),
-            pltpu.VMEM((heads, hd), F32),
-            pltpu.VMEM((heads, hd), BF16),
-            pltpu.VMEM((lines, plane, heads, hd), BF16),
-            pltpu.VMEM((lines, plane, heads, hd), BF16),
-            pltpu.VMEM((lines, plane, group, 128), F32),
-            pltpu.VMEM((plane, lines, heads, hd), BF16),
-            pltpu.VMEM((plane, lines, group, 128), F32),
-            pltpu.VMEM((lines, heads, hd), BF16),
-            pltpu.VMEM((lines, group, 128), F32),
-            pltpu.VMEM((lines, heads, hd), BF16),
-            pltpu.VMEM((lines, group, 128), F32),
-            pltpu.VMEM((2, count, hd), F32),
-            pltpu.SMEM(lengths.shape, jnp.int32),
-            pltpu.VMEM((1, count), jnp.int32),
-            pltpu.VMEM((1, count), jnp.int32),
-            pltpu.VMEM(freqs.shape, F32),
-            pltpu.VMEM(queries.shape, BF16),
-            pltpu.VMEM((1, width), F32),
-            pltpu.VMEM((1, hd), F32),
-            dma((7,)),
-            dma((4,)),
-            dma((chunks,)),
-            dma((chunks,)),
-            dma((chunks,)),
-            dma((chunks,)),
-            dma((6,)),
-            dma((6,)),
+        out_specs=(vmem, vmem, vmem, pl.BlockSpec(memory_space=pltpu.SMEM)),
+        scratch_shapes=big + [
+            pltpu.VMEM((fill, count), BF16),
+            pack,
+            pltpu.VMEM((hopped, fill, chunk), BF16),
+            pltpu.VMEM((hopped, deep, fill, chunk), BF16),
+            pltpu.VMEM((deep, half * cap, fill), BF16),
+            pltpu.VMEM((hopped, deep, half, cap, chunk), BF16),
+        ] + spread + [
+            pltpu.VMEM((1, fill), F32),
+            pltpu.VMEM((deep, 1, fill), F32),
+            pltpu.VMEM((8, 128), F32),
+            pltpu.VMEM((max(1, grps - 1), 8, 128), F32),
+        ] + loaded + sems + [
+            dma((hopped,)), dma((hopped,)), dma((hopped,)), dma((hopped,)), dma((2,)), dma((2,)),
         ],
         compiler_params=pltpu.CompilerParams(
             collective_id=0, has_side_effects=True, vmem_limit_bytes=60 * 1024 * 1024
         ),
         name="restore_attend",
-    )(
-        hidden_rows, w_key, w_value, lengths, owners.reshape(1, count), positions.reshape(1, count), freqs, queries,
-        ln_gain.reshape(1, width), k_gain.reshape(1, hd),
+    )(*inputs)
+
+    def again(*_):
+        return pl.pallas_call(
+            functools.partial(kernel, n, plane, cap, hd),
+            out_shape=(pltpu.VMEM((1, heads * hd), BF16), caches, caches),
+            in_specs=[pl.BlockSpec(memory_space=pltpu.HBM)] * 10,
+            out_specs=(vmem, vmem, vmem),
+            scratch_shapes=big + [pack] + spread + loaded + sems,
+            compiler_params=pltpu.CompilerParams(
+                collective_id=1, has_side_effects=True, vmem_limit_bytes=60 * 1024 * 1024
+            ),
+            name="restore_attend_direct",
+        )(*inputs)
+
+    attended, key_cache, value_cache = lax.cond(
+        over[0] > 0.5, again, lambda *done: done, attended, key_cache, value_cache
     )
     return attended, key_cache.reshape(n * cap, kv_width), value_cache.reshape(n * cap, kv_width)
 

time: 63.7 us -> 58.6 us (0.920)
  Pallas kernels: 60.4 us -> 55.1 us
    pallas_call x1, Pallas kernels: 60.4 us -> 55.1 us  [on_device(): pl.pallas_call(functools.partial(fast_kernel, n, plane, cap, hd, fill), o...]
    unnamed x3 -> x17, local copies, waits for them, and re-layouts: 2.56 us -> 2.59 us
where the time goes in v1:
time: 58.6 us; the launch traced here: 58.5 us
  Pallas kernels  55.1 us (94%)
  local copies, waits for them, and re-layouts  2.59 us (4%)
  between operations  0.77 us (1%)
    pallas_call x1, Pallas kernels, on_device(): pl.pallas_call(functools.partial(fast_kernel, n, plane, cap, hd, fill), o...  55.1 us
    unnamed x17, local copies, waits for them, and re-layouts  2.59 us

profile of v1, /device:TPU:0, one launch (start us, length us, event | category | flops | bytes accessed | tf_op | source)
XLA Modules:
  0.0 58.5 jit_solution(18043441819146018154)
XLA Ops:
  0.6 0.0 copy-start
  0.6 0.0 copy-start.1
  0.7 0.0 copy-start.2
  0.7 0.0 copy-start.3
  0.7 0.0 copy-start.4
  0.7 0.0 copy-start.5
  0.7 0.0 copy-start.6
  0.7 55.1 %restore_attend.1 = (bf16[1,8192]{1,0:T(2,128)(2,1)S(1)}, bf16[16,64,512]{2,1,0:T(8,128)(2,1)S(1)}, bf16[16,64,512]{2,1,0:T(8,128)(2,1)S(1)}, f32[1]{0:T(128)S(4)}) custom-call(bf16[512,4096]{1,0:T(8,128)(2,1)} %x_ref.1, bf16[4096,512]{1,0:T(8,128)(2,1)} %wk_ref.1, bf16[4096,512]{1,0:T(8,128)(2,1)} %wv_ref.1, s32[4]{0:T(128)} %len_in.1, s32[1,512]{1,0:T(1,128)} %bitcast.11, ...), custom_call_target="tpu_custom_call" | custom-call | tf_op jit(solution)/shard_map/restore_attend/pallas_call | solution.py:696
  55.9 0.0 copy-done
  55.9 0.0 copy-done.1
  55.9 0.0 copy-done.2
  55.9 0.0 copy-done.3
  55.9 0.0 copy-done.4
  55.9 0.0 copy-done.5
  55.9 0.0 copy-done.6
  55.9 1.0 %copy.24 = bf16[1024,512]{1,0:T(8,128)(2,1)} copy(bf16[1024,512]{1,0:T(8,128)(2,1)S(1)} %bitcast.8) | data formatting | bytes 2097152
  56.9 1.0 %copy.23 = bf16[1024,512]{1,0:T(8,128)(2,1)} copy(bf16[1024,512]{1,0:T(8,128)(2,1)S(1)} %bitcast.7) | data formatting | bytes 2097152
  57.9 0.6 %copy.22 = bf16[1,8192]{1,0:T(2,128)(2,1)} copy(bf16[1,8192]{1,0:T(2,128)(2,1)S(1)} %get-tuple-element.70) | data formatting | bytes 32768
  (1 shorter events, 0.0 us)
Async XLA Ops:
  0.6 55.2 %copy-start = (bf16[1,8192]{1,0:T(2,128)(2,1)S(1)}, bf16[1,8192]{1,0:T(2,128)(2,1)}, u32[]{:S(2)}) copy-start(bf16[1,8192]{1,0:T(2,128)(2,1)} %q_in.1) | copy-start | bytes 49156
  0.6 55.2 %copy-start.1 = (f32[64,1]{1,0:T(8,128)S(1)}, f32[64,1]{1,0:T(8,128)}, u32[]{:S(2)}) copy-start(f32[64,1]{1,0:T(8,128)} %constant.5.clone.freq_in) | copy-start | bytes 772
  0.7 55.2 %copy-start.2 = (f32[4096]{0:T(1024)S(1)}, f32[4096]{0:T(1024)}, u32[]{:S(2)}) copy-start(f32[4096]{0:T(1024)} %param.17) | copy-start | bytes 49156
  0.7 55.2 %copy-start.3 = (s32[512,1]{0,1:T(1,128)S(1)}, s32[512,1]{0,1:T(1,128)}, u32[]{:S(2)}) copy-start(s32[512,1]{0,1:T(1,128)} %param.14) | copy-start | bytes 6148
  0.7 55.2 %copy-start.4 = (s32[512]{0:T(512)S(1)}, s32[512]{0:T(512)}, u32[]{:S(2)}) copy-start(s32[512]{0:T(512)} %param.13) | copy-start | bytes 6148
  0.7 55.2 %copy-start.5 = (s32[4]{0:T(128)S(1)}, s32[4]{0:T(128)}, u32[]{:S(2)}) copy-start(s32[4]{0:T(128)} %len_in.1) | copy-start | bytes 52
  0.7 55.2 %copy-start.6 = (f32[128]{0:T(128)S(1)}, f32[128]{0:T(128)}, u32[]{:S(2)}) copy-start(f32[128]{0:T(128)} %param.20) | copy-start | bytes 1540

commit v2 on v1

--- a/solution.py
+++ b/solution.py
@@ -23,6 +23,17 @@
         out = out + bit * (p + q - 2 * p * q)
         bit *= 2
     return out
+
+
+def settle(a_in, k_in, v_in, a_out, k_out, v_out, sem):
+    copies = [
+        pltpu.make_async_copy(src, dst, sem.at[i])
+        for i, (src, dst) in enumerate(((k_in, k_out), (v_in, v_out), (a_in, a_out)))
+    ]
+    for copy in copies:
+        copy.start()
+    for copy in copies:
+        copy.wait()
 
 
 def fast_kernel(n, plane, cap, hd, fill, x_ref, wk_ref, wv_ref, len_in, own_in, pos_in, freq_in, q_in, gain_in, kg_in,
@@ -188,8 +199,13 @@
         out_ref, cols = target(c)
         packed = jnp.dot(onehot[...], kv[c], preferred_element_type=F32)
         pack[c] = packed.reshape(n, cap, chunk).astype(BF16)
-        every(lambda d: send(pack.at[c, d], out_ref.at[me, :, cols], kv_send.at[c], kv_recv.at[c], d))
+        beside(lambda d: send(pack.at[c, d], out_ref.at[me, :, cols], kv_send.at[c], kv_recv.at[c], d))
         keep(c)
+
+    def cross(c):
+        out_ref, cols = target(c)
+        loop(half + 1, lambda i: send(
+            pack.at[c, xor(me, n - i, n)], out_ref.at[me, :, cols], kv_send.at[c], kv_recv.at[c], xor(me, n - i, n)))
 
     def forward(c):
         out_ref, cols = target(c)
@@ -246,8 +262,7 @@
     turn[1] = jnp.concatenate([-sine, sine], axis=0).T
     for c in range(per, chunks):
         project(c)
-        if c < hopped:
-            hop(c)
+        hop(c) if c < hopped else ship(c)
 
     row = me * rows + lax.broadcasted_iota(jnp.int32, (1, rows), 1)
     convs = len_ref.shape[0]
@@ -301,6 +316,7 @@
     pa[spot] = part[:, spot]
     sa[spot] = stat[:, spot]
     forward(0)
+    forward(1)
 
     def merge(count, p_at, s_at):
         top = lax.fori_loop(0, count, lambda s, t: jnp.maximum(t, s_at(s)), jnp.full((group, 128), MASKED, F32))
@@ -339,8 +355,8 @@
     pb[line] = mid_p[line]
     sb[line] = mid_s[line]
     for c in range(hopped, chunks):
-        ship(c)
-    for c in range(1, hopped):
+        cross(c)
+    for c in range(2, hopped):
         forward(c)
     whole(pb.at[pl.ds(0, lines - 1)], hop_recv.at[4])
     whole(sb.at[pl.ds(0, lines - 1)], hop_recv.at[5])
@@ -735,6 +751,19 @@
     attended, key_cache, value_cache = lax.cond(
         over[0] > 0.5, again, lambda *done: done, attended, key_cache, value_cache
     )
+    hbm = pl.BlockSpec(memory_space=pltpu.HBM)
+    attended, key_cache, value_cache = pl.pallas_call(
+        settle,
+        out_shape=(
+            jax.ShapeDtypeStruct((1, heads * hd), BF16),
+            jax.ShapeDtypeStruct((n, cap, kv_width), BF16),
+            jax.ShapeDtypeStruct((n, cap, kv_width), BF16),
+        ),
+        in_specs=[vmem] * 3,
+        out_specs=(hbm, hbm, hbm),
+        scratch_shapes=[dma((3,))],
+        name="settle",
+    )(attended, key_cache, value_cache)
     return attended, key_cache.reshape(n * cap, kv_width), value_cache.reshape(n * cap, kv_width)
 
 

time: 58.6 us -> 56.9 us (0.971)
  local copies, waits for them, and re-layouts: 2.59 us -> 0.03 us
    unnamed x17 -> x14, local copies, waits for them, and re-layouts: 2.59 us -> 0.03 us
    pallas_call x0 -> x1, Pallas kernels: none -> 1.35 us  [on_device(): pl.pallas_call(settle, out_shape=(jax.ShapeDtypeStruct((1, heads * hd), B...]
    pallas_call x1, Pallas kernels: 55.1 us -> 54.3 us  [on_device(): pl.pallas_call(functools.partial(fast_kernel, n, plane, cap, hd, fill), o...]
where the time goes in v2:
time: 56.9 us; the launch traced here: 56.7 us
  Pallas kernels  55.6 us (98%)
  between operations  0.92 us (2%)
    pallas_call x1, Pallas kernels, on_device(): pl.pallas_call(functools.partial(fast_kernel, n, plane, cap, hd, fill), o...  54.3 us
    pallas_call x1, Pallas kernels, on_device(): pl.pallas_call(settle, out_shape=(jax.ShapeDtypeStruct((1, heads * hd), B...  1.35 us

profile of v2, /device:TPU:0, one launch (start us, length us, event | category | flops | bytes accessed | tf_op | source)
XLA Modules:
  0.0 56.7 jit_solution(1002090677317228188)
XLA Ops:
  0.6 0.0 copy-start
  0.6 0.0 copy-start.1
  0.7 0.0 copy-start.2
  0.7 0.0 copy-start.3
  0.7 0.0 copy-start.4
  0.7 0.0 copy-start.5
  0.7 0.0 copy-start.6
  0.7 54.3 %restore_attend.1 = (bf16[1,8192]{1,0:T(2,128)(2,1)S(1)}, bf16[16,64,512]{2,1,0:T(8,128)(2,1)S(1)}, bf16[16,64,512]{2,1,0:T(8,128)(2,1)S(1)}, f32[1]{0:T(128)S(4)}) custom-call(bf16[512,4096]{1,0:T(8,128)(2,1)} %x_ref.1, bf16[4096,512]{1,0:T(8,128)(2,1)} %wk_ref.1, bf16[4096,512]{1,0:T(8,128)(2,1)} %wv_ref.1, s32[4]{0:T(128)} %len_in.1, s32[1,512]{1,0:T(1,128)} %bitcast.9, ...), custom_call_target="tpu_custom_call" | custom-call | tf_op jit(solution)/shard_map/restore_attend/pallas_call | solution.py:712
  55.0 0.0 copy-done
  55.0 0.0 copy-done.1
  55.0 0.0 copy-done.2
  55.0 0.0 copy-done.3
  55.0 0.0 copy-done.4
  55.0 0.0 copy-done.5
  55.0 0.0 copy-done.6
  55.0 0.2 conditional.1
  55.2 1.3 %settle.1 = (bf16[1,8192]{1,0:T(2,128)(2,1)}, bf16[16,64,512]{2,1,0:T(8,128)(2,1)}, bf16[16,64,512]{2,1,0:T(8,128)(2,1)}) custom-call(bf16[1,8192]{1,0:T(2,128)(2,1)S(1)} %get-tuple-element.53.a_in, bf16[16,64,512]{2,1,0:T(8,128)(2,1)S(1)} %get-tuple-element.54.k_in, bf16[16,64,512]{2,1,0:T(8,128)(2,1)S(1)} %get-tuple-element.55.v_in), custom_call_target="tpu_custom_call" | custom-call | tf_op jit(solution)/shard_map/settle/pallas_call | solution.py:755
Async XLA Ops:
  0.6 54.3 %copy-start = (bf16[1,8192]{1,0:T(2,128)(2,1)S(1)}, bf16[1,8192]{1,0:T(2,128)(2,1)}, u32[]{:S(2)}) copy-start(bf16[1,8192]{1,0:T(2,128)(2,1)} %q_in.1) | copy-start | bytes 49156
  0.6 54.3 %copy-start.1 = (f32[64,1]{1,0:T(8,128)S(1)}, f32[64,1]{1,0:T(8,128)}, u32[]{:S(2)}) copy-start(f32[64,1]{1,0:T(8,128)} %constant.5.clone.freq_in) | copy-start | bytes 772
  0.7 54.3 %copy-start.2 = (f32[4096]{0:T(1024)S(1)}, f32[4096]{0:T(1024)}, u32[]{:S(2)}) copy-start(f32[4096]{0:T(1024)} %param.17) | copy-start | bytes 49156
  0.7 54.3 %copy-start.3 = (s32[512,1]{0,1:T(1,128)S(1)}, s32[512,1]{0,1:T(1,128)}, u32[]{:S(2)}) copy-start(s32[512,1]{0,1:T(1,128)} %param.14) | copy-start | bytes 6148
  0.7 54.3 %copy-start.4 = (s32[512]{0:T(512)S(1)}, s32[512]{0:T(512)}, u32[]{:S(2)}) copy-start(s32[512]{0:T(512)} %param.13) | copy-start | bytes 6148
  0.7 54.3 %copy-start.5 = (s32[4]{0:T(128)S(1)}, s32[4]{0:T(128)}, u32[]{:S(2)}) copy-start(s32[4]{0:T(128)} %len_in.1) | copy-start | bytes 52
  0.7 54.3 %copy-start.6 = (f32[128]{0:T(128)S(1)}, f32[128]{0:T(128)}, u32[]{:S(2)}) copy-start(f32[128]{0:T(128)} %param.20) | copy-start | bytes 1540
